TPU v7x, 32 devices: a whole 2x2x4 slice. The times are simulated.
32 devices in a mesh: seq: 16 (over z, y, x), head: 2 (over core).
Axes of the slice: x: 2, y: 2, z: 4, core: 2. Of those that a mesh axis runs over, the one named last changes fastest.
Arguments:
- queries: bfloat16 [4096, 4096], P('seq', 'head'), may hold values from -12 to 12
- key_input: bfloat16 [4096, 4096], P('seq', 'head'), may hold values from -1.796875 to 1.796875
- value_input: bfloat16 [4096, 4096], P('seq', 'head'), may hold values from -32 to 32
- norm_gain: bfloat16 [4096], P('head'), may hold values from 0.099609375 to 1.8984375
- out_weight: bfloat16 [4096, 3072], P('head', 'seq'), may hold values from -0.125 to 0.125
- target: bfloat16 [4096, 3072], P('seq', 'head'), may hold values from -6 to 6
Outputs:
- output: bfloat16 [4096, 3072], P('seq', 'head')
- query_grad: bfloat16 [4096, 4096], P('seq', 'head')
- key_grad: bfloat16 [4096, 4096], P('seq', 'head')
- value_grad: bfloat16 [4096, 4096], P('seq', 'head')
- gain_grads: float32 [16, 4096], P('seq', 'head')
- weight_grads: bfloat16 [16, 4096, 3072], P('seq', 'head')
All inputs are finite; a program needn't handle non-finite values.
Results may differ from a plain program's by a relative error of at most 0.022.
Values may be sent and summed in bfloat16 or wider, within the bound.
A program may use at most 128 MiB of HBM per device.

v0:
```python
import jax
import jax.numpy as jnp
from jax import lax
from jax.sharding import PartitionSpec as P

HEAD_DIM = 128
FEATURES = 4096
EPSILON = 1e-06


def entering(shard, axis, backward):
    count = lax.axis_size(axis)
    pieces = shard.astype(jnp.bfloat16).reshape(count, -1, shard.shape[-1])
    spread = lax.all_to_all(pieces, axis, 0, 0)
    row_index = lax.broadcasted_iota(jnp.int32, (count, count), 0)
    col_index = lax.broadcasted_iota(jnp.int32, (count, count), 1)
    chosen = col_index > row_index if backward else col_index < row_index
    sums = jnp.einsum(
        "ij,jrc->irc", chosen.astype(jnp.bfloat16), spread, preferred_element_type=jnp.float32
    )
    return lax.all_to_all(sums.astype(jnp.bfloat16), axis, 0, 0).reshape(shard.shape)


def causal(count):
    row_index = lax.broadcasted_iota(jnp.int32, (count, count), 0)
    col_index = lax.broadcasted_iota(jnp.int32, (count, count), 1)
    return row_index >= col_index


def per_device(queries, key_input, value_input, norm_gain, out_weight, target):
    tok_count = queries.shape[0]
    local_heads = queries.shape[1] // HEAD_DIM
    shape3 = (tok_count, local_heads, HEAD_DIM)
    q_heads = queries.reshape(shape3)
    k_heads = key_input.reshape(shape3)
    v_heads = value_input.reshape(shape3)
    keep_mask = causal(tok_count)
    f32 = jnp.float32
    state_local = jnp.einsum("shd,she->hde", k_heads, v_heads, preferred_element_type=f32)
    state_low = entering(state_local, "seq", False)
    scores = jnp.einsum("thd,shd->hts", q_heads, k_heads, preferred_element_type=f32)
    scores_low = jnp.where(keep_mask[None], scores, 0.0).astype(jnp.bfloat16)
    attended = jnp.einsum("hts,shd->thd", scores_low, v_heads, preferred_element_type=f32)
    attended = attended + jnp.einsum("thd,hde->the", q_heads, state_low, preferred_element_type=f32)
    mixed = attended.reshape(tok_count, -1)
    gain_float = norm_gain.astype(f32)
    squares = lax.psum(jnp.sum(mixed * mixed, axis=1, keepdims=True), "head")
    inverse = lax.rsqrt(squares / FEATURES + EPSILON)
    normed = (mixed * inverse * gain_float).astype(jnp.bfloat16)
    full_weight = lax.all_gather(out_weight, "seq", axis=1, tiled=True)
    partial_value = jnp.dot(normed, full_weight, preferred_element_type=f32)
    projected = lax.psum_scatter(
        partial_value.astype(jnp.bfloat16), "head", scatter_dimension=1, tiled=True
    ).astype(jnp.float32)
    output = projected.astype(jnp.bfloat16)
    grad_local = (projected - target.astype(f32)).astype(jnp.bfloat16)
    out_grad = lax.all_gather(grad_local, "head", axis=1, tiled=True)
    normed_grad = lax.dot_general(
        out_grad, full_weight, (((1,), (1,)), ((), ())), preferred_element_type=f32
    )
    product = jnp.sum(grad_local.astype(f32) * projected, axis=1, keepdims=True)
    inner = lax.psum(product, "head") / inverse
    mixed_grad = inverse * gain_float * normed_grad - mixed * inverse**3 * inner / FEATURES
    mixed_grad = mixed_grad.astype(jnp.bfloat16)
    gain_grads = jnp.sum(normed_grad * mixed * inverse, axis=0)[None]
    weight_grads = lax.dot_general(
        normed, out_grad, (((0,), (0,)), ((), ())), preferred_element_type=f32
    ).astype(jnp.bfloat16)[None]
    grad_heads = mixed_grad.reshape(shape3)
    grad_state = jnp.einsum("thd,the->hde", q_heads, grad_heads, preferred_element_type=f32)
    later_low = entering(grad_state, "seq", True)
    pairs = jnp.einsum("thd,shd->hts", grad_heads, v_heads, preferred_element_type=f32)
    pairs_low = jnp.where(keep_mask[None], pairs, 0.0).astype(jnp.bfloat16)
    query_grad = jnp.einsum("hts,shd->thd", pairs_low, k_heads, preferred_element_type=f32)
    query_grad = query_grad + jnp.einsum(
        "the,hde->thd", grad_heads, state_low, preferred_element_type=f32
    )
    key_grad = jnp.einsum("hts,thd->shd", pairs_low, q_heads, preferred_element_type=f32)
    key_grad = key_grad + jnp.einsum("she,hde->shd", v_heads, later_low, preferred_element_type=f32)
    value_grad = jnp.einsum("hts,the->she", scores_low, grad_heads, preferred_element_type=f32)
    value_grad = value_grad + jnp.einsum(
        "shd,hde->she", k_heads, later_low, preferred_element_type=f32
    )
    flat_shape = (tok_count, -1)
    return (
        output,
        query_grad.reshape(flat_shape).astype(jnp.bfloat16),
        key_grad.reshape(flat_shape).astype(jnp.bfloat16),
        value_grad.reshape(flat_shape).astype(jnp.bfloat16),
        gain_grads,
        weight_grads,
    )


def solution(mesh):
    placed = (
        P("seq", "head"),
        P("seq", "head"),
        P("seq", "head"),
        P("head"),
        P("head", "seq"),
        P("seq", "head"),
    )
    return jax.shard_map(
        per_device,
        mesh=mesh,
        in_specs=placed,
        out_specs=(
            P("seq", "head"),
            P("seq", "head"),
            P("seq", "head"),
            P("seq", "head"),
            P("seq", "head"),
            P("seq", "head", None),
        ),
        check_vma=False,
    )
```

profile of v0, /device:TPU:0, one launch (start us, length us, event | category | flops | bytes accessed | tf_op | source)
XLA Modules:
  0.0 288.4 jit_solution(15459992873029129070)
XLA Ops:
  7.9 2.5 copy.91
  10.4 1.6 copy.59
  12.5 30.5 %all_to_all.20 = bf16[16,128,128]{2,1,0:T(8,128)(2,1)S(1)} all-to-all(bf16[16,128,128]{2,1,0:T(8,128)(2,1)S(1)} %convolution_convert_fusion.4), channel_id=1, replica_groups=mesh['seq'=16,'head'=2] {'seq'}, dimensions={0} | all-to-all | bytes 1048576 | tf_op jit(solution)/shard_map/all_to_all | solution.py:14
  44.4 8.5 %all-to-all-start.1 = ((bf16[16,128,128]{2,1,0:T(8,128)(2,1)}), bf16[16,128,128]{2,1,0:T(8,128)(2,1)S(1)}, u32[]{:S(2)}, u32[]{:S(2)}) async-start(bf16[16,128,128]{2,1,0:T(8,128)(2,1)} %copy.62), calls=%async_computation.1 | async-start | bytes 1048576 | tf_op jit(solution)/shard_map/all_to_all | solution.py:21
  53.0 1.9 select_convert_fusion.1
  56.3 2.2 fusion.5
  58.4 14.0 %all-to-all-done.1 = bf16[16,128,128]{2,1,0:T(8,128)(2,1)S(1)} async-done(((bf16[16,128,128]{2,1,0:T(8,128)(2,1)}), bf16[16,128,128]{2,1,0:T(8,128)(2,1)S(1)}, u32[]{:S(2)}, u32[]{:S(2)}) %all-to-all-start.1) | async-done | bytes 524320 | tf_op jit(solution)/shard_map/all_to_all | solution.py:21
  72.4 3.6 %multiply_reduce_fusion.1 = (f32[256]{0:T(256)S(1)}, f32[256,16,128]{0,2,1:T(8,128)}) fusion(bf16[16,128,128]{2,1,0:T(8,128)(2,1)S(1)} %all-to-all-done.1, f32[16,256,128]{1,2,0:T(8,128)} %fusion.5, bf16[256,2048]{1,0:T(8,128)(2,1)S(1)} %copy-done), kind=kOutput, calls=%fused_computation.13 | convolution fusion | flops 135790336 | bytes 5768192 | tf_op jit(solution)/shard_map/thd,hde->the/dot_general | solution.py:44
  76.0 1.9 copy.65
  78.0 2.5 psum.14
  80.5 96.6 %all-gather.3.cloned.1.call-done = bf16[2048,3072]{0,1:T(8,128)(2,1)} async-done(((bf16[2048,192]{0,1:T(8,128)(2,1)}), bf16[2048,3072]{0,1:T(8,128)(2,1)}) %all-gather.3.cloned.1.call-update) | async-done | bytes 12582928 | tf_op jit(solution)/shard_map/all_gather | solution.py:50
  177.0 14.0 %convolution_convert_fusion = bf16[256,3072]{1,0:T(8,128)(2,1)} fusion(bf16[2048,3072]{0,1:T(8,128)(2,1)} %all-gather.3.cloned.1.call-done, f32[256,2048]{1,0:T(8,128)S(1)} %copy.65, f32[2048]{0:T(1024)S(1)} %convert_element_type.75, f32[256]{0:T(256)S(1)} %bitcast.127), kind=kOutput, calls=%fused_computation.3 | convolution fusion | flops 3223584768 | bytes 16262144 | tf_op jit(solution)/shard_map/dot_general | solution.py:51
  191.1 7.2 %reduce-scatter.2.cloned.1.call-done = bf16[256,1536]{1,0:T(8,128)(2,1)} async-done(((bf16[256,3072]{1,0:T(8,128)(2,1)}), bf16[256,1536]{1,0:T(8,128)(2,1)}) %reduce-scatter.2.cloned.1.call-update) | async-done | bytes 786448 | tf_op jit(solution)/shard_map/reduce_scatter | solution.py:52
  198.4 2.5 fusion.3
  200.9 2.7 psum.15
  203.6 8.6 %all-gather.5.cloned.1.call-done = bf16[256,3072]{1,0:T(8,128)(2,1)} async-done(((bf16[256,1536]{1,0:T(8,128)(2,1)}), bf16[256,3072]{1,0:T(8,128)(2,1)}) %all-gather.5.cloned.1.call-update) | async-done | bytes 1572880 | tf_op jit(solution)/shard_map/all_gather | solution.py:57
  212.2 10.4 %multiply_reduce_fusion = (f32[2048]{0:T(1024)}, bf16[256,2048]{1,0:T(8,128)(2,1)}) fusion(f32[256,2048]{1,0:T(8,128)S(1)} %copy.65, f32[256]{0:T(256)S(1)} %bitcast.128, f32[256]{0:T(256)S(1)} %bitcast.133, f32[256]{0:T(256)S(1)} %bitcast.132, f32[2048]{0:T(1024)S(1)} %convert_element_type.75, bf16[256,3072]{1,0:T(8,128)(2,1)} %all-gather.5.cloned.1.call-done, ...), kind=kOutput, calls=%fused_computation.9 | convolution fusion | flops 3226466304 | bytes 17320960 | tf_op jit(solution)/shard_map/dot_general | solution.py:58
  222.6 1.6 copy.87
  225.4 2.1 select_convert_fusion
  227.5 2.1 copy.74
  229.7 6.8 %all-to-all-start.2 = ((bf16[16,128,128]{2,1,0:T(8,128)(2,1)}), bf16[16,128,128]{2,1,0:T(8,128)(2,1)}, u32[]{:S(2)}, u32[]{:S(2)}) async-start(bf16[16,128,128]{2,1,0:T(8,128)(2,1)} %copy.74), calls=%async_computation.3 | async-start | bytes 1048576 | tf_op jit(solution)/shard_map/all_to_all | solution.py:14
  236.5 2.5 fusion.33
  240.9 3.4 %fusion.34 = f32[16,128,256]{2,1,0:T(8,128)} fusion(bf16[256,16,128]{0,2,1:T(8,128)(2,1)S(1)} %bitcast.120, bf16[16,256,256]{2,1,0:T(8,128)(2,1)} %copy-done.8), kind=kOutput, calls=%fused_computation.55 | convolution fusion | flops 268435456 | bytes 5242880 | tf_op jit(solution)/shard_map/hts,the->she/dot_general | solution.py:80
  244.3 7.8 %all-to-all-done.2 = bf16[16,128,128]{2,1,0:T(8,128)(2,1)} async-done(((bf16[16,128,128]{2,1,0:T(8,128)(2,1)}), bf16[16,128,128]{2,1,0:T(8,128)(2,1)}, u32[]{:S(2)}, u32[]{:S(2)}) %all-to-all-start.2) | async-done | bytes 524320 | tf_op jit(solution)/shard_map/all_to_all | solution.py:14
  252.0 1.4 convolution_convert_fusion.1
  254.4 4.2 %all-to-all-start.3 = ((bf16[16,128,128]{2,1,0:T(8,128)(2,1)}), bf16[16,128,128]{2,1,0:T(8,128)(2,1)}, u32[]{:S(2)}, u32[]{:S(2)}) async-start(bf16[16,128,128]{2,1,0:T(8,128)(2,1)} %copy.76), calls=%async_computation.4 | async-start | bytes 1048576 | tf_op jit(solution)/shard_map/all_to_all | solution.py:21
  258.7 1.9 fusion.12
  261.5 6.7 %convert_bitcast_fusion = bf16[1,2048,3072]{2,1,0:T(8,128)(2,1)} fusion(bf16[256,3072]{1,0:T(8,128)(2,1)S(1)} %copy-done.13, f32[256,2048]{1,0:T(8,128)S(1)} %copy-done.2, f32[2048]{0:T(1024)S(1)} %convert_element_type.75, f32[256]{0:T(256)S(1)} %bitcast.129), kind=kOutput, calls=%fused_computation | convolution fusion | flops 3229089792 | bytes 16262144 | tf_op jit(solution)/shard_map/dot_general | solution.py:66
  268.2 4.8 %all-to-all-done.3 = bf16[16,128,128]{2,1,0:T(8,128)(2,1)} async-done(((bf16[16,128,128]{2,1,0:T(8,128)(2,1)}), bf16[16,128,128]{2,1,0:T(8,128)(2,1)}, u32[]{:S(2)}, u32[]{:S(2)}) %all-to-all-start.3) | async-done | bytes 524320 | tf_op jit(solution)/shard_map/all_to_all | solution.py:21
  273.0 2.9 add_convert_fusion
  275.9 2.4 copy.84
  278.2 2.2 fusion
  (48 shorter events, 10.4 us)
Async XLA Ops:
  7.2 45.9 %copy-start = (bf16[256,2048]{1,0:T(8,128)(2,1)S(1)}, bf16[256,2048]{1,0:T(8,128)(2,1)}, u32[]{:S(2)}) copy-start(bf16[256,2048]{1,0:T(8,128)(2,1)} %param.6) | copy-start | bytes 3145732
  7.2 169.8 %all-gather.3.cloned.1.call-start = ((), (), s32[]{:S(2)}) async-start(), calls=%async_computation.5 | async-start | bytes 13369344 | tf_op jit(solution)/shard_map/all_gather | solution.py:50
  7.9 4.2 %copy-start.5 = (bf16[256,2048]{1,0:T(8,128)(2,1)S(1)}, bf16[256,2048]{1,0:T(8,128)(2,1)}, u32[]{:S(2)}) copy-start(bf16[256,2048]{1,0:T(8,128)(2,1)} %param.8) | copy-start | bytes 3145732
  12.1 31.4 %copy-start.3 = (bf16[256,16,128]{0,2,1:T(8,128)(2,1)}, bf16[256,16,128]{0,2,1:T(8,128)(2,1)S(1)}, u32[]{:S(2)}) copy-start(bf16[256,16,128]{0,2,1:T(8,128)(2,1)S(1)} %copy.59) | copy-start | bytes 3145732
  12.5 40.4 %copy-start.14 = (bf16[2048]{0:T(1024)(128)(2,1)S(1)}, bf16[2048]{0:T(1024)(128)(2,1)}, u32[]{:S(2)}) copy-start(bf16[2048]{0:T(1024)(128)(2,1)} %param.9) | copy-start | bytes 12292
  44.4 28.0 %all-to-all-start.1 = ((bf16[16,128,128]{2,1,0:T(8,128)(2,1)}), bf16[16,128,128]{2,1,0:T(8,128)(2,1)S(1)}, u32[]{:S(2)}, u32[]{:S(2)}) async-start(bf16[16,128,128]{2,1,0:T(8,128)(2,1)} %copy.62), calls=%async_computation.1 | async-start | bytes 1048576 | tf_op jit(solution)/shard_map/all_to_all | solution.py:21
  52.9 145.5 %reduce-scatter.2.cloned.1.call-start = ((), (), s32[]{:S(2)}) async-start(), calls=%async_computation.6 | async-start | bytes 2359296 | tf_op jit(solution)/shard_map/reduce_scatter | solution.py:52
  55.0 1.3 copy-start.8
  72.4 3.6 %copy-start.11 = (bf16[16,128,128]{2,1,0:T(8,128)(2,1)}, bf16[16,128,128]{2,1,0:T(8,128)(2,1)S(1)}, u32[]{:S(2)}) copy-start(bf16[16,128,128]{2,1,0:T(8,128)(2,1)S(1)} %all-to-all-done.1) | copy-start | bytes 1572868
  78.0 134.2 %copy-start.1 = (f32[256,2048]{1,0:T(8,128)}, f32[256,2048]{1,0:T(8,128)S(1)}, u32[]{:S(2)}) copy-start(f32[256,2048]{1,0:T(8,128)S(1)} %copy.65) | copy-start | bytes 6291460
  191.1 21.1 %all-gather.5.cloned.1.call-start = ((), (), s32[]{:S(2)}) async-start(), calls=%async_computation.7 | async-start | bytes 2359296 | tf_op jit(solution)/shard_map/all_gather | solution.py:57
  222.6 2.8 copy-start.6
  227.5 9.0 %copy-start.4 = (bf16[256,16,128]{0,2,1:T(8,128)(2,1)S(1)}, bf16[256,16,128]{0,2,1:T(8,128)(2,1)}, u32[]{:S(2)}) copy-start(bf16[256,16,128]{0,2,1:T(8,128)(2,1)} %copy-done.3) | copy-start | bytes 3145732
  229.7 22.4 %all-to-all-start.2 = ((bf16[16,128,128]{2,1,0:T(8,128)(2,1)}), bf16[16,128,128]{2,1,0:T(8,128)(2,1)}, u32[]{:S(2)}, u32[]{:S(2)}) async-start(bf16[16,128,128]{2,1,0:T(8,128)(2,1)} %copy.74), calls=%async_computation.3 | async-start | bytes 1048576 | tf_op jit(solution)/shard_map/all_to_all | solution.py:14
  236.5 2.5 copy-start.12
  244.2 14.4 %copy-start.9 = (bf16[16,256,256]{2,1,0:T(8,128)(2,1)S(1)}, bf16[16,256,256]{2,1,0:T(8,128)(2,1)}, u32[]{:S(2)}) copy-start(bf16[16,256,256]{2,1,0:T(8,128)(2,1)} %select_convert_fusion) | copy-start | bytes 6291460
  254.4 18.6 %all-to-all-start.3 = ((bf16[16,128,128]{2,1,0:T(8,128)(2,1)}), bf16[16,128,128]{2,1,0:T(8,128)(2,1)}, u32[]{:S(2)}, u32[]{:S(2)}) async-start(bf16[16,128,128]{2,1,0:T(8,128)(2,1)} %copy.76), calls=%async_computation.4 | async-start | bytes 1048576 | tf_op jit(solution)/shard_map/all_to_all | solution.py:21
  258.7 1.9 copy-start.2
  258.7 2.8 copy-start.13
  261.5 11.5 %copy-start.10 = (f32[16,128,256]{2,1,0:T(8,128)S(1)}, f32[16,128,256]{2,1,0:T(8,128)}, u32[]{:S(2)}) copy-start(f32[16,128,256]{2,1,0:T(8,128)} %fusion.34) | copy-start | bytes 6291460
  275.9 2.4 copy-start.7
Sparse Core Ops, SparseCore 0:
  10.8 166.2 all-gather.2
  191.2 7.1 reduce-scatter.1
  201.0 11.0 all-gather.4
where the time goes:
time: 289 us; the launch traced here: 288 us
  waiting for transfers between devices  140 us (48%)
  matrix products  57.7 us (20%)
  blocking collectives  35.6 us (12%)
  starting transfers between devices  19.7 us (7%)
  local copies, waits for them, and re-layouts  19.1 us (7%)
  between operations  14 us (5%)
    all_gather x1, waiting for transfers between devices, per_device(): full_weight = lax.all_gather(out_weight, 'seq', axis=1, tiled=True)  96.6 us
    all_to_all x1, blocking collectives, entering(): spread = lax.all_to_all(pieces, axis, 0, 0)  30.5 us
    all_to_all x2, waiting for transfers between devices, entering(): lax.all_to_all(sums.astype(jnp.bfloat16), axis, 0, 0).reshape(shard.shape)  18.8 us
    dot_general x1, matrix products, per_device(): partial_value = jnp.dot(normed, full_weight, preferred_element_type=f32)  14 us
    all_to_all x2, starting transfers between devices, entering(): lax.all_to_all(sums.astype(jnp.bfloat16), axis, 0, 0).reshape(shard.shape)  12.7 us
    dot_general x1, matrix products, per_device(): lax.dot_general(out_grad, full_weight, (((1,), (1,)), ((), ())), preferre...  10.4 us
    unnamed x34, local copies, waits for them, and re-layouts  10 us
    all_gather x1, waiting for transfers between devices, per_device(): out_grad = lax.all_gather(grad_local, 'head', axis=1, tiled=True)  8.6 us
  transfers between devices with their start and end apart: 6, of which 6 were waited for; matrix products, arithmetic and copies ran while one was open for 11% of the time, Pallas kernels for 0%

commit v1 on v0

--- a/solution.py
+++ b/solution.py
@@ -47,7 +47,7 @@
     squares = lax.psum(jnp.sum(mixed * mixed, axis=1, keepdims=True), "head")
     inverse = lax.rsqrt(squares / FEATURES + EPSILON)
     normed = (mixed * inverse * gain_float).astype(jnp.bfloat16)
-    full_weight = lax.all_gather(out_weight, "seq", axis=1, tiled=True)
+    full_weight = jnp.concatenate(lax.all_gather(out_weight, "seq"), axis=1)
     partial_value = jnp.dot(normed, full_weight, preferred_element_type=f32)
     projected = lax.psum_scatter(
         partial_value.astype(jnp.bfloat16), "head", scatter_dimension=1, tiled=True

time: 289 us -> 321 us (1.11)
  local copies, waits for them, and re-layouts: 19.1 us -> 48 us
    reshape x0 -> x1, local copies, waits for them, and re-layouts: none -> 18.3 us  [per_device(): full_weight = jnp.concatenate(lax.all_gather(out_weight, 'seq'), axis=1)]
    unnamed x34 -> x31, local copies, waits for them, and re-layouts: 10 us -> 21.7 us
    all_gather x1, waiting for transfers between devices: 96.6 us -> 101 us  [per_device(): full_weight = jnp.concatenate(lax.all_gather(out_weight, 'seq'), axis=1)]
  transfers between devices with their start and end apart: 6 -> 6, of which waited for: 6 -> 6; matrix products, arithmetic and copies ran while one was open for 11% -> 10% of each run, Pallas kernels for 0% -> 0%
where the time goes in v1:
time: 321 us; the launch traced here: 320 us
  waiting for transfers between devices  141 us (44%)
  matrix products  56.7 us (18%)
  local copies, waits for them, and re-layouts  48 us (15%)
  blocking collectives  35.8 us (11%)
  starting transfers between devices  19.9 us (6%)
  between operations  14 us (4%)
  other arithmetic  3.89 us (1%)
    all_gather x1, waiting for transfers between devices, per_device(): full_weight = jnp.concatenate(lax.all_gather(out_weight, 'seq'), axis=1)  101 us
    all_to_all x1, blocking collectives, entering(): spread = lax.all_to_all(pieces, axis, 0, 0)  30.5 us
    unnamed x31, local copies, waits for them, and re-layouts  21.7 us
    all_to_all x2, waiting for transfers between devices, entering(): lax.all_to_all(sums.astype(jnp.bfloat16), axis, 0, 0).reshape(shard.shape)  19.3 us
    reshape x1, local copies, waits for them, and re-layouts, per_device(): full_weight = jnp.concatenate(lax.all_gather(out_weight, 'seq'), axis=1)  18.3 us
    dot_general x1, matrix products, per_device(): partial_value = jnp.dot(normed, full_weight, preferred_element_type=f32)  14 us
    all_to_all x2, starting transfers between devices, entering(): lax.all_to_all(sums.astype(jnp.bfloat16), axis, 0, 0).reshape(shard.shape)  13 us
    dot_general x1, matrix products, per_device(): lax.dot_general(out_grad, full_weight, (((1,), (1,)), ((), ())), preferre...  10 us
  transfers between devices with their start and end apart: 6, of which 6 were waited for; matrix products, arithmetic and copies ran while one was open for 10% of the time, Pallas kernels for 0%

profile of v1, /device:TPU:0, one launch (start us, length us, event | category | flops | bytes accessed | tf_op | source)
XLA Modules:
  0.0 319.9 jit_solution(15544852751830114839)
XLA Ops:
  7.9 2.5 copy.120
  10.4 1.6 copy.88
  12.5 30.5 %all_to_all.20 = bf16[16,128,128]{2,1,0:T(8,128)(2,1)S(1)} all-to-all(bf16[16,128,128]{2,1,0:T(8,128)(2,1)S(1)} %convolution_convert_fusion.4), channel_id=1, replica_groups=mesh['seq'=16,'head'=2] {'seq'}, dimensions={0} | all-to-all | bytes 1048576 | tf_op jit(solution)/shard_map/all_to_all | solution.py:14
  44.4 8.7 %all-to-all-start.1 = ((bf16[16,128,128]{2,1,0:T(8,128)(2,1)}), bf16[16,128,128]{2,1,0:T(8,128)(2,1)}, u32[]{:S(2)}, u32[]{:S(2)}) async-start(bf16[16,128,128]{2,1,0:T(8,128)(2,1)} %copy.91), calls=%async_computation.1 | async-start | bytes 1048576 | tf_op jit(solution)/shard_map/all_to_all | solution.py:21
  53.3 1.9 select_convert_fusion.1
  56.6 2.2 fusion.5
  58.7 14.4 %all-to-all-done.1 = bf16[16,128,128]{2,1,0:T(8,128)(2,1)} async-done(((bf16[16,128,128]{2,1,0:T(8,128)(2,1)}), bf16[16,128,128]{2,1,0:T(8,128)(2,1)}, u32[]{:S(2)}, u32[]{:S(2)}) %all-to-all-start.1) | async-done | bytes 524320 | tf_op jit(solution)/shard_map/all_to_all | solution.py:21
  73.2 2.3 multiply_reduce_fusion.1
  75.5 2.7 psum.14
  79.4 100.7 %all-gather.6.cloned.1.call-done = bf16[32768,192]{0,1:T(8,128)(2,1)} async-done(((bf16[2048,192]{0,1:T(8,128)(2,1)}), bf16[32768,192]{0,1:T(8,128)(2,1)}) %all-gather.6.cloned.1.call-update) | async-done | bytes 12582928 | tf_op jit(solution)/shard_map/all_gather | solution.py:50
  180.2 11.7 %copy.121 = bf16[24,8,16,2048]{3,2,1,0:T(8,128)(2,1)S(1)} copy(bf16[24,8,16,2048]{3,1,2,0:T(8,128)(2,1)} %bitcast.135) | data formatting | bytes 25165824
  191.9 18.3 %copy.94 = bf16[2048,16,192]{0,2,1:T(8,128)(2,1)} copy(bf16[2048,16,192]{0,1,2:T(8,128)(2,1)S(1)} %bitcast.129) | data formatting | bytes 25165824 | tf_op jit(solution)/shard_map/reshape | solution.py:50
  210.1 14.0 %convolution_convert_fusion = bf16[256,3072]{1,0:T(8,128)(2,1)} fusion(bf16[256,2048]{0,1:T(8,128)(2,1)S(1)} %bitcast.143, bf16[2048,3072]{0,1:T(8,128)(2,1)} %bitcast.136), kind=kOutput, calls=%fused_computation.3 | convolution fusion | flops 3222011904 | bytes 15204352 | tf_op jit(solution)/shard_map/dot_general | solution.py:51
  224.2 7.2 %reduce-scatter.2.cloned.1.call-done = bf16[256,1536]{1,0:T(8,128)(2,1)} async-done(((bf16[256,3072]{1,0:T(8,128)(2,1)}), bf16[256,1536]{1,0:T(8,128)(2,1)}) %reduce-scatter.2.cloned.1.call-update) | async-done | bytes 786448 | tf_op jit(solution)/shard_map/reduce_scatter | solution.py:52
  231.4 2.5 fusion.3
  234.0 1.8 copy.95
  235.8 2.7 psum.15
  238.5 6.7 %all-gather.4.cloned.1.call-done = bf16[256,3072]{1,0:T(8,128)(2,1)} async-done(((bf16[256,1536]{1,0:T(8,128)(2,1)}), bf16[256,3072]{1,0:T(8,128)(2,1)}) %all-gather.4.cloned.1.call-update) | async-done | bytes 1572880 | tf_op jit(solution)/shard_map/all_gather | solution.py:57
  245.2 10.0 %multiply_reduce_fusion = (f32[2048]{0:T(1024)}, bf16[256,2048]{1,0:T(8,128)(2,1)S(1)}) fusion(f32[256,2048]{1,0:T(8,128)} %copy.95, f32[256]{0:T(256)S(1)} %bitcast.145, f32[256]{0:T(256)S(1)} %bitcast.150, f32[256]{0:T(256)S(1)} %bitcast.149, f32[2048]{0:T(1024)S(1)} %get-tuple-element.36, bf16[256,3072]{1,0:T(8,128)(2,1)} %all-gather.4.cloned.1.call-done, ...), kind=kOutput, calls=%fused_computation.10 | convolution fusion | flops 3226466304 | bytes 17320960 | tf_op jit(solution)/shard_map/dot_general | solution.py:58
  257.0 2.1 select_convert_fusion
  259.1 6.8 %all-to-all-start.2 = ((bf16[16,128,128]{1,2,0:T(8,128)(2,1)}), bf16[16,128,128]{1,2,0:T(8,128)(2,1)}, u32[]{:S(2)}, u32[]{:S(2)}) async-start(bf16[16,128,128]{1,2,0:T(8,128)(2,1)} %fusion.4), calls=%async_computation.3 | async-start | bytes 1048576 | tf_op jit(solution)/shard_map/all_to_all | solution.py:14
  265.9 2.4 fusion.35
  271.3 3.4 %fusion.36 = f32[16,128,256]{2,1,0:T(8,128)} fusion(bf16[256,16,128]{0,2,1:T(8,128)(2,1)S(1)} %bitcast.134, bf16[16,256,256]{2,1,0:T(8,128)(2,1)} %copy-done.7), kind=kOutput, calls=%fused_computation.59 | convolution fusion | flops 268435456 | bytes 5242880 | tf_op jit(solution)/shard_map/hts,the->she/dot_general | solution.py:80
  274.6 6.8 %all-to-all-done.2 = bf16[16,128,128]{1,2,0:T(8,128)(2,1)} async-done(((bf16[16,128,128]{1,2,0:T(8,128)(2,1)}), bf16[16,128,128]{1,2,0:T(8,128)(2,1)}, u32[]{:S(2)}, u32[]{:S(2)}) %all-to-all-start.2) | async-done | bytes 524320 | tf_op jit(solution)/shard_map/all_to_all | solution.py:14
  281.5 2.2 copy.103
  286.0 4.2 %all-to-all-start.3 = ((bf16[16,128,128]{2,1,0:T(8,128)(2,1)}), bf16[16,128,128]{2,1,0:T(8,128)(2,1)}, u32[]{:S(2)}, u32[]{:S(2)}) async-start(bf16[16,128,128]{2,1,0:T(8,128)(2,1)} %copy.104), calls=%async_computation.4 | async-start | bytes 1048576 | tf_op jit(solution)/shard_map/all_to_all | solution.py:21
  290.2 1.9 fusion.12
  293.0 6.7 %convert_bitcast_fusion = bf16[1,2048,3072]{2,1,0:T(8,128)(2,1)} fusion(bf16[256,3072]{1,0:T(8,128)(2,1)S(1)} %copy-done.10, f32[256,2048]{1,0:T(8,128)S(1)} %copy-done.1, f32[2048]{0:T(1024)S(1)} %get-tuple-element.36, f32[256]{0:T(256)S(1)} %bitcast.146), kind=kOutput, calls=%fused_computation | convolution fusion | flops 3229089792 | bytes 16262144 | tf_op jit(solution)/shard_map/dot_general | solution.py:66
  299.7 4.8 %all-to-all-done.3 = bf16[16,128,128]{2,1,0:T(8,128)(2,1)} async-done(((bf16[16,128,128]{2,1,0:T(8,128)(2,1)}), bf16[16,128,128]{2,1,0:T(8,128)(2,1)}, u32[]{:S(2)}, u32[]{:S(2)}) %all-to-all-start.3) | async-done | bytes 524320 | tf_op jit(solution)/shard_map/all_to_all | solution.py:21
  304.5 2.8 add_convert_fusion
  307.4 2.4 copy.113
  309.7 2.2 fusion
  (47 shorter events, 14.6 us)
Async XLA Ops:
  7.2 46.1 %copy-start = (bf16[256,2048]{1,0:T(8,128)(2,1)S(1)}, bf16[256,2048]{1,0:T(8,128)(2,1)}, u32[]{:S(2)}) copy-start(bf16[256,2048]{1,0:T(8,128)(2,1)} %param.6) | copy-start | bytes 3145732
  7.2 173.0 %all-gather.6.cloned.1.call-start = ((), (), s32[]{:S(2)}) async-start(), calls=%async_computation.7 | async-start | bytes 13369344 | tf_op jit(solution)/shard_map/all_gather | solution.py:50
  7.9 4.2 %copy-start.4 = (bf16[256,2048]{1,0:T(8,128)(2,1)S(1)}, bf16[256,2048]{1,0:T(8,128)(2,1)}, u32[]{:S(2)}) copy-start(bf16[256,2048]{1,0:T(8,128)(2,1)} %param.8) | copy-start | bytes 3145732
  12.1 31.4 %copy-start.2 = (bf16[256,16,128]{0,2,1:T(8,128)(2,1)}, bf16[256,16,128]{0,2,1:T(8,128)(2,1)S(1)}, u32[]{:S(2)}) copy-start(bf16[256,16,128]{0,2,1:T(8,128)(2,1)S(1)} %copy.88) | copy-start | bytes 3145732
  12.5 40.7 %copy-start.12 = (bf16[2048]{0:T(1024)(128)(2,1)S(1)}, bf16[2048]{0:T(1024)(128)(2,1)}, u32[]{:S(2)}) copy-start(bf16[2048]{0:T(1024)(128)(2,1)} %param.9) | copy-start | bytes 12292
  44.4 28.7 %all-to-all-start.1 = ((bf16[16,128,128]{2,1,0:T(8,128)(2,1)}), bf16[16,128,128]{2,1,0:T(8,128)(2,1)}, u32[]{:S(2)}, u32[]{:S(2)}) async-start(bf16[16,128,128]{2,1,0:T(8,128)(2,1)} %copy.91), calls=%async_computation.1 | async-start | bytes 1048576 | tf_op jit(solution)/shard_map/all_to_all | solution.py:21
  53.2 178.3 %reduce-scatter.2.cloned.1.call-start = ((), (), s32[]{:S(2)}) async-start(), calls=%async_computation.5 | async-start | bytes 2359296 | tf_op jit(solution)/shard_map/reduce_scatter | solution.py:52
  55.2 1.3 copy-start.7
  191.9 18.3 %copy-start.11 = (bf16[256,16,128]{0,2,1:T(8,128)(2,1)S(1)}, bf16[256,16,128]{0,2,1:T(8,128)(2,1)}, u32[]{:S(2)}) copy-start(bf16[256,16,128]{0,2,1:T(8,128)(2,1)} %multiply_convert_fusion.1) | copy-start | bytes 3145732
  224.2 21.1 %all-gather.4.cloned.1.call-start = ((), (), s32[]{:S(2)}) async-start(), calls=%async_computation.6 | async-start | bytes 2359296 | tf_op jit(solution)/shard_map/all_gather | solution.py:57
  255.7 1.2 copy-start.5
  257.0 9.0 %copy-start.3 = (bf16[256,16,128]{0,2,1:T(8,128)(2,1)S(1)}, bf16[256,16,128]{0,2,1:T(8,128)(2,1)}, u32[]{:S(2)}) copy-start(bf16[256,16,128]{0,2,1:T(8,128)(2,1)} %copy-done.2) | copy-start | bytes 3145732
  259.1 22.4 %all-to-all-start.2 = ((bf16[16,128,128]{1,2,0:T(8,128)(2,1)}), bf16[16,128,128]{1,2,0:T(8,128)(2,1)}, u32[]{:S(2)}, u32[]{:S(2)}) async-start(bf16[16,128,128]{1,2,0:T(8,128)(2,1)} %fusion.4), calls=%async_computation.3 | async-start | bytes 1048576 | tf_op jit(solution)/shard_map/all_to_all | solution.py:14
  274.6 15.6 %copy-start.8 = (bf16[16,256,256]{2,1,0:T(8,128)(2,1)S(1)}, bf16[16,256,256]{2,1,0:T(8,128)(2,1)}, u32[]{:S(2)}) copy-start(bf16[16,256,256]{2,1,0:T(8,128)(2,1)} %select_convert_fusion) | copy-start | bytes 6291460
  286.0 18.6 %all-to-all-start.3 = ((bf16[16,128,128]{2,1,0:T(8,128)(2,1)}), bf16[16,128,128]{2,1,0:T(8,128)(2,1)}, u32[]{:S(2)}, u32[]{:S(2)}) async-start(bf16[16,128,128]{2,1,0:T(8,128)(2,1)} %copy.104), calls=%async_computation.4 | async-start | bytes 1048576 | tf_op jit(solution)/shard_map/all_to_all | solution.py:21
  290.2 1.9 copy-start.1
  290.2 2.8 copy-start.10
  293.0 11.5 %copy-start.9 = (f32[16,128,256]{2,1,0:T(8,128)S(1)}, f32[16,128,256]{2,1,0:T(8,128)}, u32[]{:S(2)}) copy-start(f32[16,128,256]{2,1,0:T(8,128)} %fusion.36) | copy-start | bytes 6291460
  307.4 2.4 copy-start.6
Sparse Core Ops, SparseCore 0:
  10.7 169.3 all-gather.5
  224.3 7.0 reduce-scatter.1
  234.1 11.0 all-gather.3
